TPU v7x, 512 devices: a whole 4x8x8 slice. The times are simulated.
512 devices in a mesh: gx: 64 (over z_lo, y, core), gy: 8 (over x, z_hi).
Axes of the slice: x: 4, y: 8, z: 8 (z_hi: 2, z_lo: 4; z = z_hi * 4 + z_lo), core: 2. Of those that a mesh axis runs over, the one named last changes fastest.
Arguments:
- velocity: float32 [3, 512, 256, 128], P(None, 'gx', 'gy'), may hold values from -6 to 6
- stress: float32 [6, 512, 256, 128], P(None, 'gx', 'gy'), may hold values from -6 to 6
- lame_lambda: bfloat16 [512, 256, 128], P('gx', 'gy'), may hold values from 0.5 to 1.5
- shear_modulus: bfloat16 [512, 256, 128], P('gx', 'gy'), may hold values from 0.29882812 to 1
- buoyancy: bfloat16 [512, 256, 128], P('gx', 'gy'), may hold values from 0.5 to 1.5
- source_p: bfloat16 [3, 512, 256, 128], P(None, 'gx', 'gy'), may hold values from -6 to 6
- source_s: bfloat16 [3, 512, 256, 128], P(None, 'gx', 'gy'), may hold values from -6 to 6
Outputs:
- image_p: float32 [512, 256, 128], P('gx', 'gy')
- image_s: float32 [512, 256, 128], P('gx', 'gy')
All inputs are finite; a program needn't handle non-finite values.
Results may differ from a plain program's by a relative error of at most 0.0003.
Values sent between devices are 32-bit elements; how exact they have to be, the bound alone decides.
A program may use at most 64 MiB of HBM per device.

v0:
```python
import math
import jax
import jax.numpy as jnp
from jax import lax
from jax.sharding import PartitionSpec as P

STEPS = 2
time_step = 0.2


def passed_along(block, axis, distance):
    devices = range(lax.axis_size(axis))
    route = [(i - distance, i) for i in devices if i - distance in devices]
    return lax.ppermute(block, axis, route)


def x_rims(planes, offset):
    return passed_along(planes, "gx", offset)


def y_rims(planes, offset):
    return passed_along(planes, "gy", offset)


def with_next(field, rim, which):
    length = field.shape[which]
    return jnp.concatenate([lax.slice_in_dim(field, 1, length, axis=which), rim], axis=which)


def with_prior(field, rim, which):
    length = field.shape[which]
    return jnp.concatenate([rim, lax.slice_in_dim(field, 0, length - 1, axis=which)], axis=which)


def zero_rim(field, which):
    return jnp.zeros_like(lax.slice_in_dim(field, 0, 1, axis=which))


def stress_step(velocity, stress, lame_value, shear_value):
    x_speed, y_speed, z_speed = (velocity[0], velocity[1], velocity[2])
    prior_x = x_rims(x_speed[None, -1:], 1)
    next_x = x_rims(jnp.stack([y_speed[:1], z_speed[:1]]), -1)
    prior_y = y_rims(y_speed[None, :, -1:], 1)
    next_y = y_rims(jnp.stack([x_speed[:, :1], z_speed[:, :1]]), -1)
    strain_x = x_speed - with_prior(x_speed, prior_x[0], 0)
    strain_y = y_speed - with_prior(y_speed, prior_y[0], 1)
    strain_z = z_speed - with_prior(z_speed, zero_rim(z_speed, 2), 2)
    volume = strain_x + strain_y + strain_z
    normal_x = stress[0] + time_step * (lame_value * volume + 2.0 * shear_value * strain_x)
    normal_y = stress[1] + time_step * (lame_value * volume + 2.0 * shear_value * strain_y)
    normal_z = stress[2] + time_step * (lame_value * volume + 2.0 * shear_value * strain_z)
    shear_xy = stress[3] + time_step * shear_value * (
        with_next(x_speed, next_y[0], 1) - x_speed + (with_next(y_speed, next_x[0], 0) - y_speed)
    )
    shear_xz = stress[4] + time_step * shear_value * (
        with_next(x_speed, zero_rim(x_speed, 2), 2)
        - x_speed
        + (with_next(z_speed, next_x[1], 0) - z_speed)
    )
    shear_yz = stress[5] + time_step * shear_value * (
        with_next(y_speed, zero_rim(y_speed, 2), 2)
        - y_speed
        + (with_next(z_speed, next_y[1], 1) - z_speed)
    )
    return jnp.stack([normal_x, normal_y, normal_z, shear_xy, shear_xz, shear_yz])


def velocity_step(velocity, stress, buoy_value):
    normal_x, normal_y, normal_z = (stress[0], stress[1], stress[2])
    shear_xy, shear_xz, shear_yz = (stress[3], stress[4], stress[5])
    next_x = x_rims(normal_x[None, :1], -1)
    prior_x = x_rims(jnp.stack([shear_xy[-1:], shear_xz[-1:]]), 1)
    next_y = y_rims(normal_y[None, :, :1], -1)
    prior_y = y_rims(jnp.stack([shear_xy[:, -1:], shear_yz[:, -1:]]), 1)
    x_speed = velocity[0] + time_step * buoy_value * (
        with_next(normal_x, next_x[0], 0)
        - normal_x
        + (shear_xy - with_prior(shear_xy, prior_y[0], 1))
        + (shear_xz - with_prior(shear_xz, zero_rim(shear_xz, 2), 2))
    )
    y_speed = velocity[1] + time_step * buoy_value * (
        shear_xy
        - with_prior(shear_xy, prior_x[0], 0)
        + (with_next(normal_y, next_y[0], 1) - normal_y)
        + (shear_yz - with_prior(shear_yz, zero_rim(shear_yz, 2), 2))
    )
    z_speed = velocity[2] + time_step * buoy_value * (
        shear_xz
        - with_prior(shear_xz, prior_x[1], 0)
        + (shear_yz - with_prior(shear_yz, prior_y[1], 1))
        + (with_next(normal_z, zero_rim(normal_z, 2), 2) - normal_z)
    )
    return jnp.stack([x_speed, y_speed, z_speed])


def phase_tables(length):
    positions = jnp.arange(length, dtype=jnp.int32)
    product = positions[:, None] * positions[None, :] % length
    phases = product.astype(jnp.float32) * (2.0 * math.pi / length)
    return (jnp.cos(phases), jnp.sin(phases))


def z_tables(z_cells, gy_count):
    quarter = z_cells // (2 * gy_count)
    width = gy_count * (quarter + 1)
    column = jnp.arange(width, dtype=jnp.int32)
    block = column // (quarter + 1)
    slot = column % (quarter + 1)
    waves = jnp.where(slot < quarter, block * quarter + slot, z_cells // 2)
    weight = jnp.where(
        slot < quarter, jnp.where(waves == 0, 1.0, 2.0), jnp.where(block == gy_count - 1, 1.0, 0.0)
    ).astype(jnp.float32)
    positions = jnp.arange(z_cells, dtype=jnp.int32)
    product = positions[:, None] * waves[None, :] % z_cells
    phases = product.astype(jnp.float32) * (2.0 * math.pi / z_cells)
    cos_fwd = jnp.cos(phases)
    sin_fwd = jnp.sin(phases)
    cos_back = jnp.transpose(cos_fwd) * weight[:, None]
    sin_back = jnp.transpose(sin_fwd) * weight[:, None]
    return (cos_fwd, sin_fwd, cos_back, sin_back, waves)


def contract(pattern, left, right):
    return jnp.einsum(pattern, left, right, precision=lax.Precision.HIGHEST)


def complex_sum(real_in, imag_in, cosine, sine, pattern, forward_sign):
    cos_real = contract(pattern, real_in, cosine)
    sin_imag = contract(pattern, imag_in, sine)
    cos_imag = contract(pattern, imag_in, cosine)
    sin_real = contract(pattern, real_in, sine)
    if forward_sign:
        return (cos_real + sin_imag, cos_imag - sin_real)
    return (cos_real - sin_imag, cos_imag + sin_real)


def signed_index(positions, length):
    half_length = length // 2
    signed = jnp.where(
        positions < half_length,
        positions,
        jnp.where(positions == half_length, 0, positions - length),
    )
    return signed.astype(jnp.float32)


def forward(velocity, cos_fwd, sin_fwd):
    x_cells, y_cells = (velocity.shape[1], velocity.shape[2])
    gx_count = lax.axis_size("gx")
    gy_count = lax.axis_size("gy")
    x_total = gx_count * x_cells
    y_total = gy_count * y_cells
    kept = cos_fwd.shape[1]
    z_part = kept // gy_count
    y_part = y_total // gx_count
    real_part = contract("cxyn,nk->ckxy", velocity, cos_fwd)
    imag_part = -contract("cxyn,nk->ckxy", velocity, sin_fwd)
    packed = jnp.stack([real_part, imag_part]).reshape(2, 3, 1, kept, x_cells * y_cells)
    arrived = lax.all_to_all(packed, "gy", split_axis=3, concat_axis=2, tiled=True)
    comp_count = arrived.shape[1]
    pieces = arrived.reshape(2, comp_count, gy_count, z_part, x_cells, y_cells)
    cos_y, sin_y = phase_tables(y_total)
    cos_y = cos_y.reshape(gy_count, y_cells, y_total)
    sin_y = sin_y.reshape(gy_count, y_cells, y_total)
    real_out, imag_out = complex_sum(pieces[0], pieces[1], cos_y, sin_y, "cgzxl,glk->ckzx", True)
    after_y = jnp.stack([real_out, imag_out]).reshape(2, comp_count, 1, y_total, z_part * x_cells)
    arrived = lax.all_to_all(after_y, "gx", split_axis=3, concat_axis=2, tiled=True)
    comp_count = arrived.shape[1]
    pieces = arrived.reshape(2, comp_count, gx_count, y_part, z_part, x_cells)
    cos_x, sin_x = phase_tables(x_total)
    cos_x = cos_x.reshape(gx_count, x_cells, x_total)
    sin_x = sin_x.reshape(gx_count, x_cells, x_total)
    real_out, imag_out = complex_sum(pieces[0], pieces[1], cos_x, sin_x, "cgazl,glk->cazk", True)
    return jnp.stack([real_out, imag_out])


def project(spectra, waves, z_total):
    y_part, z_part, x_total = (spectra.shape[2], spectra.shape[3], spectra.shape[4])
    gy_count = lax.axis_size("gy")
    y_total = y_part * lax.axis_size("gx")
    y_index = lax.axis_index("gx") * y_part + jnp.arange(y_part, dtype=jnp.int32)
    z_index = lax.dynamic_slice_in_dim(waves.reshape(gy_count, z_part), lax.axis_index("gy"), 1, 0)[
        0
    ]
    wave_x = signed_index(jnp.arange(x_total, dtype=jnp.int32), x_total)[None, None, :]
    wave_y = signed_index(y_index, y_total)[:, None, None]
    wave_z = signed_index(z_index, z_total)[None, :, None]
    inverse_norm = 1.0 / jnp.maximum(wave_x * wave_x + wave_y * wave_y + wave_z * wave_z, 1.0)
    radial = (
        wave_x * spectra[:, 0] + wave_y * spectra[:, 1] + wave_z * spectra[:, 2]
    ) * inverse_norm
    return jnp.stack([wave_x * radial, wave_y * radial, wave_z * radial], axis=1)


def inverse_fields(spectrum, x_cells, y_cells, z_cells, cos_back, sin_back):
    comp_count, y_part, z_part, x_total = (
        spectrum.shape[1],
        spectrum.shape[2],
        spectrum.shape[3],
        spectrum.shape[4],
    )
    gx_count = lax.axis_size("gx")
    gy_count = lax.axis_size("gy")
    y_total = y_part * gx_count
    norm_factor = 1.0 / (x_total * y_total * z_cells)
    cos_x, sin_x = phase_tables(x_total)
    real_part, imag_part = complex_sum(
        spectrum[0], spectrum[1], cos_x, sin_x, "cazk,kx->cxaz", False
    )
    packed = jnp.stack([real_part, imag_part]).reshape(2, comp_count, 1, x_total, y_part * z_part)
    arrived = lax.all_to_all(packed, "gx", split_axis=3, concat_axis=2, tiled=True)
    count_here = arrived.shape[1]
    pieces = arrived.reshape(2, count_here, gx_count, x_cells, y_part, z_part)
    cos_y, sin_y = phase_tables(y_total)
    cos_y = cos_y.reshape(gx_count, y_part, y_total)
    sin_y = sin_y.reshape(gx_count, y_part, y_total)
    real_out, imag_out = complex_sum(pieces[0], pieces[1], cos_y, sin_y, "cgxaz,gay->cyzx", False)
    middle = jnp.stack([real_out, imag_out]).reshape(2, count_here, 1, y_total, z_part * x_cells)
    arrived = lax.all_to_all(middle, "gy", split_axis=3, concat_axis=2, tiled=True)
    count_here = arrived.shape[1]
    pieces = arrived.reshape(2, count_here, gy_count, y_cells, z_part, x_cells)
    cos_z = cos_back.reshape(gy_count, z_part, z_cells)
    sin_z = sin_back.reshape(gy_count, z_part, z_cells)
    cos_real = contract("cgybx,gbn->cxyn", pieces[0], cos_z)
    sin_imag = contract("cgybx,gbn->cxyn", pieces[1], sin_z)
    return (cos_real - sin_imag) * norm_factor


def shards(velocity, stress, lame_lambda, shear_modulus, buoyancy, source_p, source_s):
    lame_value = lame_lambda.astype(jnp.float32)
    shear_value = shear_modulus.astype(jnp.float32)
    buoy_value = buoyancy.astype(jnp.float32)
    for step_index in range(STEPS):
        stress = stress_step(velocity, stress, lame_value, shear_value)
        velocity = velocity_step(velocity, stress, buoy_value)
    x_cells, y_cells, z_cells = (velocity.shape[1], velocity.shape[2], velocity.shape[3])
    gy_count = lax.axis_size("gy")
    cos_fwd, sin_fwd, cos_back, sin_back, waves = z_tables(z_cells, gy_count)
    spectra = forward(velocity, cos_fwd, sin_fwd)
    compression = project(spectra, waves, z_cells)
    p_field = inverse_fields(compression, x_cells, y_cells, z_cells, cos_back, sin_back)
    s_field = velocity - p_field
    image_p = jnp.sum(source_p.astype(jnp.float32) * p_field, axis=0)
    image_s = jnp.sum(source_s.astype(jnp.float32) * s_field, axis=0)
    return (image_p, image_s)


def solution(mesh):
    in_specs = (
        P(None, "gx", "gy", None),
        P(None, "gx", "gy", None),
        P("gx", "gy", None),
        P("gx", "gy", None),
        P("gx", "gy", None),
        P(None, "gx", "gy", None),
        P(None, "gx", "gy", None),
    )
    out_specs = (P("gx", "gy", None), P("gx", "gy", None))
    return jax.shard_map(shards, mesh=mesh, in_specs=in_specs, out_specs=out_specs, check_vma=False)
```

profile of v0, /device:TPU:64, one launch (start us, length us, event | category | flops | bytes accessed | tf_op | source)
XLA Modules:
  0.0 321.7 jit_solution(4998562081433264974)
XLA Ops:
  1.8 10.0 %collective-permute-start.1 = (f32[1,8,1,128]{3,1,2,0:T(8,128)S(1)}, f32[1,8,1,128]{3,1,2,0:T(8,128)S(1)}, u32[]{:S(2)}, u32[]{:S(2)}) collective-permute-start(f32[1,8,1,128]{3,1,2,0:T(8,128)S(1)} %bitcast.460), channel_id=1, source_target_pairs={{0,1},{1,2},{2,3},{3,4},{4,5},{5,6},{6,7},{8,9},{9,10},{10,11},{11... | collective-permute-start | bytes 12296 | tf_op jit(solution)/shard_map/ppermute | solution.py:14
  12.6 4.5 %collective-permute-start.4 = (f32[2,1,32,128]{3,2,1,0:T(8,128)S(1)}, f32[2,1,32,128]{3,2,1,0:T(8,128)S(1)}, u32[]{:S(2)}, u32[]{:S(2)}) collective-permute-start(f32[2,1,32,128]{3,2,1,0:T(8,128)S(1)} %stack.134), channel_id=1, source_target_pairs={{8,0},{16,8},{24,16},{32,24},{40,32},{48,40},{56,48},{64,56},{72,6... | collective-permute-start | bytes 98312 | tf_op jit(solution)/shard_map/ppermute | solution.py:14
  17.9 1.9 collective-permute-start
  19.8 1.3 collective-permute-start.3
  22.4 6.9 %collective-permute-done.3 = f32[2,8,1,128]{3,1,2,0:T(8,128)S(1)} collective-permute-done((f32[2,8,1,128]{3,1,2,0:T(8,128)S(1)}, f32[2,8,1,128]{3,1,2,0:T(8,128)S(1)}, u32[]{:S(2)}, u32[]{:S(2)}) %collective-permute-start.3) | collective-permute-done | bytes 8224 | tf_op jit(solution)/shard_map/ppermute | solution.py:14
  29.8 3.1 collective-permute-start.5
  33.2 1.9 collective-permute-start.7
  35.1 5.8 %collective-permute-start.2 = (f32[1,1,32,128]{3,2,1,0:T(8,128)S(1)}, f32[1,1,32,128]{3,2,1,0:T(8,128)S(1)}, u32[]{:S(2)}, u32[]{:S(2)}) collective-permute-start(f32[1,1,32,128]{3,2,1,0:T(8,128)S(1)} %slice_bitcast_fusion.28), channel_id=1, source_target_pairs={{8,0},{16,8},{24,16},{32,24},{40,32},{48,40},{56,48},{64,56},{72,6... | collective-permute-start | bytes 49160 | tf_op jit(solution)/shard_map/ppermute | solution.py:14
  40.8 1.3 collective-permute-start.8
  42.5 1.3 collective-permute-start.11
  43.8 6.4 %collective-permute-done.8 = f32[1,8,1,128]{3,1,2,0:T(8,128)S(1)} collective-permute-done((f32[1,8,1,128]{3,1,2,0:T(8,128)S(1)}, f32[1,8,1,128]{3,1,2,0:T(8,128)S(1)}, u32[]{:S(2)}, u32[]{:S(2)}) %collective-permute-start.8) | collective-permute-done | bytes 4128 | tf_op jit(solution)/shard_map/ppermute | solution.py:14
  50.7 1.9 collective-permute-start.12
  52.6 8.5 %collective-permute-start.9 = (f32[1,8,1,128]{3,1,2,0:T(8,128)S(1)}, f32[1,8,1,128]{3,1,2,0:T(8,128)S(1)}, u32[]{:S(2)}, u32[]{:S(2)}) collective-permute-start(f32[1,8,1,128]{3,1,2,0:T(8,128)S(1)} %bitcast.461), channel_id=1, source_target_pairs={{0,1},{1,2},{2,3},{3,4},{4,5},{5,6},{6,7},{8,9},{9,10},{10,11},{11... | collective-permute-start | bytes 12296 | tf_op jit(solution)/shard_map/ppermute | solution.py:14
  61.1 2.1 collective-permute-start.6
  63.3 5.0 %collective-permute-done.6 = f32[1,1,32,128]{3,2,1,0:T(8,128)S(1)} collective-permute-done((f32[1,1,32,128]{3,2,1,0:T(8,128)S(1)}, f32[1,1,32,128]{3,2,1,0:T(8,128)S(1)}, u32[]{:S(2)}, u32[]{:S(2)}) %collective-permute-start.6) | collective-permute-done | bytes 16416 | tf_op jit(solution)/shard_map/ppermute | solution.py:14
  68.7 5.6 %collective-permute-start.13 = (f32[2,8,1,128]{3,1,2,0:T(8,128)S(1)}, f32[2,8,1,128]{3,1,2,0:T(8,128)S(1)}, u32[]{:S(2)}, u32[]{:S(2)}) collective-permute-start(f32[2,8,1,128]{3,1,2,0:T(8,128)S(1)} %pad_maximum_fusion.15), channel_id=1, source_target_pairs={{0,1},{1,2},{2,3},{3,4},{4,5},{5,6},{6,7},{8,9},{9,10},{10,11},{11... | collective-permute-start | bytes 24584 | tf_op jit(solution)/shard_map/ppermute | solution.py:14
  74.4 1.9 collective-permute-start.14
  76.4 1.3 collective-permute-start.15
  77.8 5.8 %collective-permute-start.10 = (f32[1,1,32,128]{3,2,1,0:T(8,128)S(1)}, f32[1,1,32,128]{3,2,1,0:T(8,128)S(1)}, u32[]{:S(2)}, u32[]{:S(2)}) collective-permute-start(f32[1,1,32,128]{3,2,1,0:T(8,128)S(1)} %slice_bitcast_fusion.20), channel_id=1, source_target_pairs={{8,0},{16,8},{24,16},{32,24},{40,32},{48,40},{56,48},{64,56},{72,6... | collective-permute-start | bytes 49160 | tf_op jit(solution)/shard_map/ppermute | solution.py:14
  83.6 2.2 collective-permute-done.15
  87.9 1.2 pad_maximum_fusion.2
  89.0 8.9 %all-to-all-start = ((f32[2,3,1,72,256]{4,0,2,1,3:T(2,128)}), f32[2,3,1,72,256]{4,0,2,1,3:T(2,128)S(1)}, u32[]{:S(2)}, u32[]{:S(2)}) async-start(f32[2,3,1,72,256]{4,0,2,1,3:T(2,128)} %pad_maximum_fusion.2), calls=%async_computation | async-start | bytes 884736 | tf_op jit(solution)/shard_map/all_to_all | solution.py:159
  98.0 14.3 %all-to-all-done = f32[2,3,1,72,256]{4,0,2,1,3:T(2,128)S(1)} async-done(((f32[2,3,1,72,256]{4,0,2,1,3:T(2,128)}), f32[2,3,1,72,256]{4,0,2,1,3:T(2,128)S(1)}, u32[]{:S(2)}, u32[]{:S(2)}) %all-to-all-start) | async-done | bytes 442400 | tf_op jit(solution)/shard_map/all_to_all | solution.py:159
  112.3 1.3 slice_reduce_fusion.5
  113.9 2.9 fusion.36
  116.8 2.9 fusion.39
  120.0 2.9 fusion.24
  122.9 3.1 fusion.33
  126.4 1.8 copy.142
  128.2 8.0 %all-to-all-start.1 = ((f32[2,3,1,256,72]{4,2,1,0,3:T(1,128)}), f32[2,3,1,256,72]{4,2,1,0,3:T(1,128)S(1)}, u32[]{:S(2)}, u32[]{:S(2)}) async-start(f32[2,3,1,256,72]{4,2,1,0,3:T(1,128)} %copy.142), calls=%async_computation.1 | async-start | bytes 1572864 | tf_op jit(solution)/shard_map/all_to_all | solution.py:167
  136.4 21.7 %all-to-all-done.1 = f32[2,3,1,256,72]{4,2,1,0,3:T(1,128)S(1)} async-done(((f32[2,3,1,256,72]{4,2,1,0,3:T(1,128)}), f32[2,3,1,256,72]{4,2,1,0,3:T(1,128)S(1)}, u32[]{:S(2)}, u32[]{:S(2)}) %all-to-all-start.1) | async-done | bytes 442400 | tf_op jit(solution)/shard_map/all_to_all | solution.py:167
  158.0 2.4 slice_reduce_fusion.3
  160.4 3.7 %reshape.522 = f32[3,64,4,9,8]{4,3,0,2,1:T(8,128)} reshape(f32[3,256,72]{2,0,1:T(4,128)S(1)} %get-tuple-element.5) | data formatting | bytes 442368 | tf_op jit(solution)/shard_map/squeeze | solution.py:173
  164.1 5.4 %copy.146 = f32[3,64,4,9,8]{1,3,4,2,0:T(8,128)S(1)} copy(f32[3,64,4,9,8]{4,3,0,2,1:T(8,128)} %reshape.522) | data formatting | bytes 442368 | tf_op jit(solution)/shard_map/squeeze | solution.py:173
  169.6 3.7 %reshape.521 = f32[3,64,4,9,8]{4,3,0,2,1:T(8,128)} reshape(f32[3,256,72]{2,0,1:T(4,128)S(1)} %get-tuple-element.4) | data formatting | bytes 442368 | tf_op jit(solution)/shard_map/squeeze | solution.py:173
  173.3 5.8 %copy.144 = f32[3,64,4,9,8]{1,3,4,2,0:T(8,128)S(1)} copy(f32[3,64,4,9,8]{4,3,0,2,1:T(8,128)} %reshape.521) | data formatting | bytes 442368 | tf_op jit(solution)/shard_map/squeeze | solution.py:173
  179.1 4.9 %convolution_bitcast_fusion.2 = f32[3,4,9,512]{3,2,1,0:T(8,128)S(1)} fusion(f32[3,64,4,9,8]{1,3,4,2,0:T(8,128)S(1)} %copy.146, s32[64,8]{0,1:T(8,128)S(1)} %multiply_add_fusion), kind=kOutput, calls=%fused_computation.20 | convolution fusion | flops 343408640 | bytes 444416 | tf_op jit(solution)/shard_map/cgazl,glk->cazk/dot_general | solution.py:124
  184.0 4.9 %convolution_bitcast_fusion = f32[3,4,9,512]{3,2,1,0:T(8,128)S(1)} fusion(f32[3,64,4,9,8]{1,3,4,2,0:T(8,128)S(1)} %copy.144, s32[64,8]{0,1:T(8,128)S(1)} %multiply_add_fusion), kind=kOutput, calls=%fused_computation.18 | convolution fusion | flops 343408640 | bytes 444416 | tf_op jit(solution)/shard_map/cgazl,glk->cazk/dot_general | solution.py:124
  188.9 5.0 %fusion.49 = f32[1,3,4,9,512]{4,3,2,1,0:T(8,128)S(1)} fusion(f32[3,4,9,512]{3,2,1,0:T(8,128)S(1)} %convolution_bitcast_fusion.2, f32[3,64,4,9,8]{1,3,4,2,0:T(8,128)S(1)} %copy.144, s32[64,8]{0,1:T(8,128)S(1)} %multiply_add_fusion), kind=kOutput, calls=%fused_computation.46 | convolution fusion | flops 343463936 | bytes 665600 | tf_op jit(solution)/shard_map/cgazl,glk->cazk/dot_general | solution.py:124
  193.9 4.9 %fusion.51 = f32[1,3,4,9,512]{4,3,2,1,0:T(8,128)S(1)} fusion(f32[3,4,9,512]{3,2,1,0:T(8,128)S(1)} %convolution_bitcast_fusion, f32[3,64,4,9,8]{1,3,4,2,0:T(8,128)S(1)} %copy.146, s32[64,8]{0,1:T(8,128)S(1)} %multiply_add_fusion), kind=kOutput, calls=%fused_computation.48 | convolution fusion | flops 343463936 | bytes 665600 | tf_op jit(solution)/shard_map/cgazl,glk->cazk/dot_general | solution.py:124
  199.2 5.1 %fusion.71 = f32[512,3,4,9]{0,3,2,1:T(8,128)S(1)} fusion(f32[2,3,4,9,512]{4,3,2,1,0:T(8,128)S(1)} %pad_maximum_fusion), kind=kOutput, calls=%fused_computation.62 | convolution fusion | flops 343408640 | bytes 614400 | tf_op jit(solution)/shard_map/cazk,kx->cxaz/dot_general | solution.py:124
  204.3 5.3 %fusion.69 = f32[512,3,4,9]{0,3,2,1:T(8,128)S(1)} fusion(f32[2,3,4,9,512]{4,3,2,1,0:T(8,128)S(1)} %pad_maximum_fusion), kind=kOutput, calls=%fused_computation.60 | convolution fusion | flops 343408640 | bytes 614400 | tf_op jit(solution)/shard_map/cazk,kx->cxaz/dot_general | solution.py:124
  209.7 5.2 %fusion.43 = f32[3,512,4,9]{1,3,2,0:T(8,128)S(1)} fusion(f32[512,3,4,9]{0,3,2,1:T(8,128)S(1)} %fusion.71, f32[2,3,4,9,512]{4,3,2,1,0:T(8,128)S(1)} %pad_maximum_fusion), kind=kOutput, calls=%fused_computation.35 | convolution fusion | flops 343463936 | bytes 1007616 | tf_op jit(solution)/shard_map/cazk,kx->cxaz/dot_general | solution.py:124
  215.0 5.2 %fusion.42 = f32[3,512,4,9]{1,3,2,0:T(8,128)S(1)} fusion(f32[512,3,4,9]{0,3,2,1:T(8,128)S(1)} %fusion.69, f32[2,3,4,9,512]{4,3,2,1,0:T(8,128)S(1)} %pad_maximum_fusion), kind=kOutput, calls=%fused_computation.33 | convolution fusion | flops 343463936 | bytes 1007616 | tf_op jit(solution)/shard_map/cazk,kx->cxaz/dot_general | solution.py:124
  220.5 1.2 copy.151
  221.7 3.9 %reshape.531 = f32[64,1,1728]{2,1,0:T(1,128)} reshape(f32[512,3,1,2,36]{4,3,2,1,0:T(2,128)S(1)} %bitcast.414) | data formatting | bytes 884736
  225.6 7.6 %all-to-all-start.2 = ((f32[64,1,1728]{2,1,0:T(1,128)}), f32[64,1,1728]{2,1,0:T(1,128)S(1)}, u32[]{:S(2)}, u32[]{:S(2)}) async-start(f32[64,1,1728]{2,1,0:T(1,128)} %reshape.531), calls=%async_computation.2 | async-start | bytes 917504 | tf_op jit(solution)/shard_map/all_to_all | solution.py:211
  233.2 15.2 %all-to-all-done.2 = f32[64,1,1728]{2,1,0:T(1,128)S(1)} async-done(((f32[64,1,1728]{2,1,0:T(1,128)}), f32[64,1,1728]{2,1,0:T(1,128)S(1)}, u32[]{:S(2)}, u32[]{:S(2)}) %all-to-all-start.2) | async-done | bytes 442400 | tf_op jit(solution)/shard_map/all_to_all | solution.py:211
  248.9 1.7 reduce.12
  250.7 2.8 reshape.532
  253.4 6.2 %slice_reduce_fusion.1 = (f32[3,512,36]{2,0,1:T(4,128)}, f32[3,512,36]{2,0,1:T(4,128)}) fusion(f32[2,3,1,512,36]{4,0,2,1,3:T(2,128)S(1)} %bitcast.413), kind=kLoop, calls=%fused_computation.79 | loop fusion | bytes 884736 | tf_op jit(solution)/shard_map/slice | solution.py:217
  259.6 3.0 reshape.523
  262.6 3.0 copy.153
  265.6 3.0 reshape.524
  268.6 3.1 copy.155
  271.7 2.9 convolution_bitcast_fusion.7
  274.7 2.9 convolution_bitcast_fusion.5
  277.6 1.7 fusion.47
  279.5 1.7 fusion.45
  281.5 1.8 copy.160
  283.2 3.8 %all-to-all-start.3 = ((f32[2,3,1,256,72]{4,2,1,0,3:T(1,128)}), f32[2,3,1,256,72]{4,2,1,0,3:T(1,128)S(1)}, u32[]{:S(2)}, u32[]{:S(2)}) async-start(f32[2,3,1,256,72]{4,2,1,0,3:T(1,128)} %copy.160), calls=%async_computation.3 | async-start | bytes 1572864 | tf_op jit(solution)/shard_map/all_to_all | solution.py:219
  287.0 26.1 %all-to-all-done.3 = f32[2,3,1,256,72]{4,2,1,0,3:T(1,128)S(1)} async-done(((f32[2,3,1,256,72]{4,2,1,0,3:T(1,128)}), f32[2,3,1,256,72]{4,2,1,0,3:T(1,128)S(1)}, u32[]{:S(2)}, u32[]{:S(2)}) %all-to-all-start.3) | async-done | bytes 442400 | tf_op jit(solution)/shard_map/all_to_all | solution.py:219
  314.7 3.0 fusion.12
  317.8 3.7 %multiply_reduce_fusion = (f32[8,32,128]{2,1,0:T(8,128)}, f32[8,32,128]{2,1,0:T(8,128)}) fusion(bf16[3,8,32,128]{3,2,1,0:T(8,128)(2,1)S(1)} %copy-done.7, f32[1,8,32,128]{3,2,1,0:T(8,128)S(1)} %get-tuple-element.36, f32[1,8,32,128]{3,2,1,0:T(8,128)S(1)} %fusion.187, f32[1,8,32,128]{3,2,1,0:T(8,128)S(1)} %get-tuple-element.35, ...), kind=kOutput, calls=%fused_computation.94 | convolution fusion | flops 86088704 | bytes 1663552 | tf_op jit(solution)/shard_map/cgybx,gbn->cxyn/dot_general | solution.py:124
  (136 shorter events, 12.2 us)
Async XLA Ops:
  0.6 28.7 %copy-start = (f32[3,8,32,128]{3,2,1,0:T(8,128)S(1)}, f32[3,8,32,128]{3,2,1,0:T(8,128)}, u32[]{:S(2)}) copy-start(f32[3,8,32,128]{3,2,1,0:T(8,128)} %param.7) | copy-start | bytes 1179652
  0.6 28.7 %copy-start.3 = (bf16[8,32,128]{2,1,0:T(8,128)(2,1)S(1)}, bf16[8,32,128]{2,1,0:T(8,128)(2,1)}, u32[]{:S(2)}) copy-start(bf16[8,32,128]{2,1,0:T(8,128)(2,1)} %param.10) | copy-start | bytes 196612
  0.7 28.7 %copy-start.5 = (f32[6,8,32,128]{3,2,1,0:T(8,128)S(1)}, f32[6,8,32,128]{3,2,1,0:T(8,128)}, u32[]{:S(2)}) copy-start(f32[6,8,32,128]{3,2,1,0:T(8,128)} %param.8) | copy-start | bytes 2359300
  1.8 27.6 %copy-start.6 = (bf16[8,32,128]{2,1,0:T(8,128)(2,1)S(1)}, bf16[8,32,128]{2,1,0:T(8,128)(2,1)}, u32[]{:S(2)}) copy-start(bf16[8,32,128]{2,1,0:T(8,128)(2,1)} %param.9) | copy-start | bytes 196612
  1.8 27.6 %collective-permute-start.1 = (f32[1,8,1,128]{3,1,2,0:T(8,128)S(1)}, f32[1,8,1,128]{3,1,2,0:T(8,128)S(1)}, u32[]{:S(2)}, u32[]{:S(2)}) collective-permute-start(f32[1,8,1,128]{3,1,2,0:T(8,128)S(1)} %bitcast.460), channel_id=1, source_target_pairs={{0,1},{1,2},{2,3},{3,4},{4,5},{5,6},{6,7},{8,9},{9,10},{10,11},{11... | collective-permute-start | bytes 12296 | tf_op jit(solution)/shard_map/ppermute | solution.py:14
  12.6 16.7 %collective-permute-start.4 = (f32[2,1,32,128]{3,2,1,0:T(8,128)S(1)}, f32[2,1,32,128]{3,2,1,0:T(8,128)S(1)}, u32[]{:S(2)}, u32[]{:S(2)}) collective-permute-start(f32[2,1,32,128]{3,2,1,0:T(8,128)S(1)} %stack.134), channel_id=1, source_target_pairs={{8,0},{16,8},{24,16},{32,24},{40,32},{48,40},{56,48},{64,56},{72,6... | collective-permute-start | bytes 98312 | tf_op jit(solution)/shard_map/ppermute | solution.py:14
  17.9 11.6 %collective-permute-start = (f32[1,1,32,128]{3,2,1,0:T(8,128)S(1)}, f32[1,1,32,128]{3,2,1,0:T(8,128)S(1)}, u32[]{:S(2)}, u32[]{:S(2)}) collective-permute-start(f32[1,1,32,128]{3,2,1,0:T(8,128)S(1)} %slice.326), channel_id=1, source_target_pairs={{0,8},{8,16},{16,24},{24,32},{32,40},{40,48},{48,56},{56,64},{64,7... | collective-permute-start | bytes 49160 | tf_op jit(solution)/shard_map/ppermute | solution.py:14
  19.8 9.5 %collective-permute-start.3 = (f32[2,8,1,128]{3,1,2,0:T(8,128)S(1)}, f32[2,8,1,128]{3,1,2,0:T(8,128)S(1)}, u32[]{:S(2)}, u32[]{:S(2)}) collective-permute-start(f32[2,8,1,128]{3,1,2,0:T(8,128)S(1)} %pad_maximum_fusion.12), channel_id=1, source_target_pairs={{1,0},{2,1},{3,2},{4,3},{5,4},{6,5},{7,6},{9,8},{10,9},{11,10},{12... | collective-permute-start | bytes 24584 | tf_op jit(solution)/shard_map/ppermute | solution.py:14
  29.6 12.6 %copy-start.4 = (bf16[8,32,128]{2,1,0:T(8,128)(2,1)S(1)}, bf16[8,32,128]{2,1,0:T(8,128)(2,1)}, u32[]{:S(2)}) copy-start(bf16[8,32,128]{2,1,0:T(8,128)(2,1)} %param.11) | copy-start | bytes 196612
  29.8 12.3 %collective-permute-start.5 = (f32[2,8,1,128]{3,1,2,0:T(8,128)S(1)}, f32[2,8,1,128]{3,1,2,0:T(8,128)S(1)}, u32[]{:S(2)}, u32[]{:S(2)}) collective-permute-start(f32[2,8,1,128]{3,1,2,0:T(8,128)S(1)} %pad_maximum_fusion.13), channel_id=1, source_target_pairs={{0,1},{1,2},{2,3},{3,4},{4,5},{5,6},{6,7},{8,9},{9,10},{10,11},{11... | collective-permute-start | bytes 24584 | tf_op jit(solution)/shard_map/ppermute | solution.py:14
  33.2 9.0 %collective-permute-start.7 = (f32[2,1,32,128]{3,2,1,0:T(8,128)S(1)}, f32[2,1,32,128]{3,2,1,0:T(8,128)S(1)}, u32[]{:S(2)}, u32[]{:S(2)}) collective-permute-start(f32[2,1,32,128]{3,2,1,0:T(8,128)S(1)} %pad_maximum_fusion.9), channel_id=1, source_target_pairs={{0,8},{8,16},{16,24},{24,32},{32,40},{40,48},{48,56},{56,64},{64,7... | collective-permute-start | bytes 98312 | tf_op jit(solution)/shard_map/ppermute | solution.py:14
  35.1 7.2 %collective-permute-start.2 = (f32[1,1,32,128]{3,2,1,0:T(8,128)S(1)}, f32[1,1,32,128]{3,2,1,0:T(8,128)S(1)}, u32[]{:S(2)}, u32[]{:S(2)}) collective-permute-start(f32[1,1,32,128]{3,2,1,0:T(8,128)S(1)} %slice_bitcast_fusion.28), channel_id=1, source_target_pairs={{8,0},{16,8},{24,16},{32,24},{40,32},{48,40},{56,48},{64,56},{72,6... | collective-permute-start | bytes 49160 | tf_op jit(solution)/shard_map/ppermute | solution.py:14
  40.8 9.4 %collective-permute-start.8 = (f32[1,8,1,128]{3,1,2,0:T(8,128)S(1)}, f32[1,8,1,128]{3,1,2,0:T(8,128)S(1)}, u32[]{:S(2)}, u32[]{:S(2)}) collective-permute-start(f32[1,8,1,128]{3,1,2,0:T(8,128)S(1)} %bitcast.459), channel_id=1, source_target_pairs={{1,0},{2,1},{3,2},{4,3},{5,4},{6,5},{7,6},{9,8},{10,9},{11,10},{12... | collective-permute-start | bytes 12296 | tf_op jit(solution)/shard_map/ppermute | solution.py:14
  42.5 20.7 %collective-permute-start.11 = (f32[2,8,1,128]{3,1,2,0:T(8,128)S(1)}, f32[2,8,1,128]{3,1,2,0:T(8,128)S(1)}, u32[]{:S(2)}, u32[]{:S(2)}) collective-permute-start(f32[2,8,1,128]{3,1,2,0:T(8,128)S(1)} %pad_maximum_fusion.14), channel_id=1, source_target_pairs={{1,0},{2,1},{3,2},{4,3},{5,4},{6,5},{7,6},{9,8},{10,9},{11,10},{12... | collective-permute-start | bytes 24584 | tf_op jit(solution)/shard_map/ppermute | solution.py:14
  50.7 12.6 %collective-permute-start.12 = (f32[2,1,32,128]{3,2,1,0:T(8,128)S(1)}, f32[2,1,32,128]{3,2,1,0:T(8,128)S(1)}, u32[]{:S(2)}, u32[]{:S(2)}) collective-permute-start(f32[2,1,32,128]{3,2,1,0:T(8,128)S(1)} %pad_maximum_fusion.10), channel_id=1, source_target_pairs={{8,0},{16,8},{24,16},{32,24},{40,32},{48,40},{56,48},{64,56},{72,6... | collective-permute-start | bytes 98312 | tf_op jit(solution)/shard_map/ppermute | solution.py:14
  52.6 10.7 %collective-permute-start.9 = (f32[1,8,1,128]{3,1,2,0:T(8,128)S(1)}, f32[1,8,1,128]{3,1,2,0:T(8,128)S(1)}, u32[]{:S(2)}, u32[]{:S(2)}) collective-permute-start(f32[1,8,1,128]{3,1,2,0:T(8,128)S(1)} %bitcast.461), channel_id=1, source_target_pairs={{0,1},{1,2},{2,3},{3,4},{4,5},{5,6},{6,7},{8,9},{9,10},{10,11},{11... | collective-permute-start | bytes 12296 | tf_op jit(solution)/shard_map/ppermute | solution.py:14
  61.1 7.2 %collective-permute-start.6 = (f32[1,1,32,128]{3,2,1,0:T(8,128)S(1)}, f32[1,1,32,128]{3,2,1,0:T(8,128)S(1)}, u32[]{:S(2)}, u32[]{:S(2)}) collective-permute-start(f32[1,1,32,128]{3,2,1,0:T(8,128)S(1)} %slice_bitcast_fusion.25), channel_id=1, source_target_pairs={{0,8},{8,16},{16,24},{24,32},{32,40},{40,48},{48,56},{56,64},{64,7... | collective-permute-start | bytes 49160 | tf_op jit(solution)/shard_map/ppermute | solution.py:14
  68.7 14.8 %collective-permute-start.13 = (f32[2,8,1,128]{3,1,2,0:T(8,128)S(1)}, f32[2,8,1,128]{3,1,2,0:T(8,128)S(1)}, u32[]{:S(2)}, u32[]{:S(2)}) collective-permute-start(f32[2,8,1,128]{3,1,2,0:T(8,128)S(1)} %pad_maximum_fusion.15), channel_id=1, source_target_pairs={{0,1},{1,2},{2,3},{3,4},{4,5},{5,6},{6,7},{8,9},{9,10},{10,11},{11... | collective-permute-start | bytes 24584 | tf_op jit(solution)/shard_map/ppermute | solution.py:14
  74.4 9.1 %collective-permute-start.14 = (f32[2,1,32,128]{3,2,1,0:T(8,128)S(1)}, f32[2,1,32,128]{3,2,1,0:T(8,128)S(1)}, u32[]{:S(2)}, u32[]{:S(2)}) collective-permute-start(f32[2,1,32,128]{3,2,1,0:T(8,128)S(1)} %pad_maximum_fusion.11), channel_id=1, source_target_pairs={{0,8},{8,16},{16,24},{24,32},{32,40},{40,48},{48,56},{56,64},{64,7... | collective-permute-start | bytes 98312 | tf_op jit(solution)/shard_map/ppermute | solution.py:14
  76.4 9.4 %collective-permute-start.15 = (f32[1,8,1,128]{3,1,2,0:T(8,128)S(1)}, f32[1,8,1,128]{3,1,2,0:T(8,128)S(1)}, u32[]{:S(2)}, u32[]{:S(2)}) collective-permute-start(f32[1,8,1,128]{3,1,2,0:T(8,128)S(1)} %bitcast.462), channel_id=1, source_target_pairs={{1,0},{2,1},{3,2},{4,3},{5,4},{6,5},{7,6},{9,8},{10,9},{11,10},{12... | collective-permute-start | bytes 12296 | tf_op jit(solution)/shard_map/ppermute | solution.py:14
  77.8 8.1 %collective-permute-start.10 = (f32[1,1,32,128]{3,2,1,0:T(8,128)S(1)}, f32[1,1,32,128]{3,2,1,0:T(8,128)S(1)}, u32[]{:S(2)}, u32[]{:S(2)}) collective-permute-start(f32[1,1,32,128]{3,2,1,0:T(8,128)S(1)} %slice_bitcast_fusion.20), channel_id=1, source_target_pairs={{8,0},{16,8},{24,16},{32,24},{40,32},{48,40},{56,48},{64,56},{72,6... | collective-permute-start | bytes 49160 | tf_op jit(solution)/shard_map/ppermute | solution.py:14
  89.0 23.3 %all-to-all-start = ((f32[2,3,1,72,256]{4,0,2,1,3:T(2,128)}), f32[2,3,1,72,256]{4,0,2,1,3:T(2,128)S(1)}, u32[]{:S(2)}, u32[]{:S(2)}) async-start(f32[2,3,1,72,256]{4,0,2,1,3:T(2,128)} %pad_maximum_fusion.2), calls=%async_computation | async-start | bytes 884736 | tf_op jit(solution)/shard_map/all_to_all | solution.py:159
  128.2 29.9 %all-to-all-start.1 = ((f32[2,3,1,256,72]{4,2,1,0,3:T(1,128)}), f32[2,3,1,256,72]{4,2,1,0,3:T(1,128)S(1)}, u32[]{:S(2)}, u32[]{:S(2)}) async-start(f32[2,3,1,256,72]{4,2,1,0,3:T(1,128)} %copy.142), calls=%async_computation.1 | async-start | bytes 1572864 | tf_op jit(solution)/shard_map/all_to_all | solution.py:167
  225.6 22.8 %all-to-all-start.2 = ((f32[64,1,1728]{2,1,0:T(1,128)}), f32[64,1,1728]{2,1,0:T(1,128)S(1)}, u32[]{:S(2)}, u32[]{:S(2)}) async-start(f32[64,1,1728]{2,1,0:T(1,128)} %reshape.531), calls=%async_computation.2 | async-start | bytes 917504 | tf_op jit(solution)/shard_map/all_to_all | solution.py:211
  271.7 5.9 %copy-start.2 = (f32[3,64,8,4,9]{1,4,3,2,0:T(8,128)S(1)}, f32[3,64,8,4,9]{1,4,3,2,0:T(8,128)}, u32[]{:S(2)}) copy-start(f32[3,64,8,4,9]{1,4,3,2,0:T(8,128)} %copy.155) | copy-start | bytes 663556
  274.7 4.9 %copy-start.1 = (f32[3,64,8,4,9]{1,4,3,2,0:T(8,128)S(1)}, f32[3,64,8,4,9]{1,4,3,2,0:T(8,128)}, u32[]{:S(2)}) copy-start(f32[3,64,8,4,9]{1,4,3,2,0:T(8,128)} %copy.153) | copy-start | bytes 663556
  283.2 29.9 %all-to-all-start.3 = ((f32[2,3,1,256,72]{4,2,1,0,3:T(1,128)}), f32[2,3,1,256,72]{4,2,1,0,3:T(1,128)S(1)}, u32[]{:S(2)}, u32[]{:S(2)}) async-start(f32[2,3,1,256,72]{4,2,1,0,3:T(1,128)} %copy.160), calls=%async_computation.3 | async-start | bytes 1572864 | tf_op jit(solution)/shard_map/all_to_all | solution.py:219
  314.5 3.3 %copy-start.7 = (bf16[3,8,32,128]{3,2,1,0:T(8,128)(2,1)S(1)}, bf16[3,8,32,128]{3,2,1,0:T(8,128)(2,1)}, u32[]{:S(2)}) copy-start(bf16[3,8,32,128]{3,2,1,0:T(8,128)(2,1)} %param.13) | copy-start | bytes 589828
  314.5 3.3 %copy-start.8 = (bf16[3,8,32,128]{3,2,1,0:T(8,128)(2,1)S(1)}, bf16[3,8,32,128]{3,2,1,0:T(8,128)(2,1)}, u32[]{:S(2)}) copy-start(bf16[3,8,32,128]{3,2,1,0:T(8,128)(2,1)} %param.12) | copy-start | bytes 589828
where the time goes:
time: 327 us; the launch traced here: 322 us
  waiting for transfers between devices  97.8 us (30%)
  starting transfers between devices  86.4 us (26%)
  matrix products  69.8 us (21%)
  local copies, waits for them, and re-layouts  60.5 us (19%)
  other arithmetic  5.12 us (2%)
    dot_general x20, matrix products, contract(): return jnp.einsum(pattern, left, right, precision=lax.Precision.HIGHEST)  69.8 us
    ppermute x16, starting transfers between devices, passed_along(): return lax.ppermute(block, axis, route)  58.2 us
    all_to_all x1, waiting for transfers between devices, inverse_fields(): lax.all_to_all(middle, 'gy', split_axis=3, concat_axis=2, tiled=True)  26.1 us
    all_to_all x1, waiting for transfers between devices, forward(): lax.all_to_all(after_y, 'gx', split_axis=3, concat_axis=2, tiled=True)  21.7 us
    ppermute x16, waiting for transfers between devices, passed_along(): return lax.ppermute(block, axis, route)  20.6 us
    all_to_all x1, waiting for transfers between devices, inverse_fields(): lax.all_to_all(packed, 'gx', split_axis=3, concat_axis=2, tiled=True)  15.2 us
    all_to_all x1, waiting for transfers between devices, forward(): lax.all_to_all(packed, 'gy', split_axis=3, concat_axis=2, tiled=True)  14.3 us
    squeeze x3, local copies, waits for them, and re-layouts, forward(): pieces[0]  9.83 us
  transfers between devices with their start and end apart: 20, of which 9 were waited for; matrix products, arithmetic and copies ran while one was open for 1% of the time, Pallas kernels for 0%

commit v1 on v0

--- a/solution.py
+++ b/solution.py
@@ -1,3 +1,4 @@
+import functools
 import math
 import jax
 import jax.numpy as jnp
@@ -6,6 +7,18 @@
 
 STEPS = 2
 time_step = 0.2
+
+
+def bands_run(values, ax_name, in_dim, where_dim):
+    return jnp.concatenate(
+        jax.lax.all_to_all(
+            jnp.stack(jnp.split(values, jax.lax.axis_size(ax_name), axis=in_dim)), ax_name, 0, 0
+        ),
+        axis=where_dim,
+    )
+
+
+open_hubs = functools.partial(bands_run, ax_name="gy", in_dim=3, where_dim=2)
 
 
 def passed_along(block, axis, distance):
@@ -216,7 +229,7 @@
     sin_y = sin_y.reshape(gx_count, y_part, y_total)
     real_out, imag_out = complex_sum(pieces[0], pieces[1], cos_y, sin_y, "cgxaz,gay->cyzx", False)
     middle = jnp.stack([real_out, imag_out]).reshape(2, count_here, 1, y_total, z_part * x_cells)
-    arrived = lax.all_to_all(middle, "gy", split_axis=3, concat_axis=2, tiled=True)
+    arrived = open_hubs(middle)
     count_here = arrived.shape[1]
     pieces = arrived.reshape(2, count_here, gy_count, y_cells, z_part, x_cells)
     cos_z = cos_back.reshape(gy_count, z_part, z_cells)

time: 327 us -> 331 us (1.012)
  local copies, waits for them, and re-layouts: 60.5 us -> 63.9 us
    unnamed x20 -> x27, local copies, waits for them, and re-layouts: 6.72 us -> 11.3 us
    slice x4 -> x1, local copies, waits for them, and re-layouts: 7.3 us -> 6.2 us  [inverse_fields(): pieces[1]]
where the time goes in v1:
time: 331 us; the launch traced here: 325 us
  waiting for transfers between devices  97.8 us (30%)
  starting transfers between devices  86.4 us (26%)
  matrix products  69.4 us (21%)
  local copies, waits for them, and re-layouts  63.9 us (19%)
  other arithmetic  5.51 us (2%)
    dot_general x20, matrix products, contract(): return jnp.einsum(pattern, left, right, precision=lax.Precision.HIGHEST)  69.4 us
    ppermute x16, starting transfers between devices, passed_along(): return lax.ppermute(block, axis, route)  58.2 us
    all_to_all x1, waiting for transfers between devices, bands_run(): jax.lax.all_to_all(jnp.stack(jnp.split(values, jax.lax.axis_size(ax_name)...  26.1 us
    all_to_all x1, waiting for transfers between devices, forward(): lax.all_to_all(after_y, 'gx', split_axis=3, concat_axis=2, tiled=True)  21.7 us
    ppermute x16, waiting for transfers between devices, passed_along(): return lax.ppermute(block, axis, route)  20.6 us
    all_to_all x1, waiting for transfers between devices, inverse_fields(): lax.all_to_all(packed, 'gx', split_axis=3, concat_axis=2, tiled=True)  15.2 us
    all_to_all x1, waiting for transfers between devices, forward(): lax.all_to_all(packed, 'gy', split_axis=3, concat_axis=2, tiled=True)  14.3 us
    unnamed x27, local copies, waits for them, and re-layouts  11.3 us
  transfers between devices with their start and end apart: 20, of which 9 were waited for; matrix products, arithmetic and copies ran while one was open for 1% of the time, Pallas kernels for 0%

profile of v1, /device:TPU:64, one launch (start us, length us, event | category | flops | bytes accessed | tf_op | source)
XLA Modules:
  0.0 325.2 jit_solution(3533298656468392771)
XLA Ops:
  0.7 1.2 slice_bitcast_fusion.9
  1.8 10.0 %collective-permute-start.1 = (f32[1,8,1,128]{3,1,2,0:T(8,128)S(1)}, f32[1,8,1,128]{3,1,2,0:T(8,128)S(1)}, u32[]{:S(2)}, u32[]{:S(2)}) collective-permute-start(f32[1,8,1,128]{3,1,2,0:T(8,128)S(1)} %bitcast.474), channel_id=1, source_target_pairs={{0,1},{1,2},{2,3},{3,4},{4,5},{5,6},{6,7},{8,9},{9,10},{10,11},{11... | collective-permute-start | bytes 12296 | tf_op jit(solution)/shard_map/ppermute | solution.py:27
  12.6 4.5 %collective-permute-start.4 = (f32[2,1,32,128]{3,2,1,0:T(8,128)S(1)}, f32[2,1,32,128]{3,2,1,0:T(8,128)S(1)}, u32[]{:S(2)}, u32[]{:S(2)}) collective-permute-start(f32[2,1,32,128]{3,2,1,0:T(8,128)S(1)} %stack.161), channel_id=1, source_target_pairs={{8,0},{16,8},{24,16},{32,24},{40,32},{48,40},{56,48},{64,56},{72,6... | collective-permute-start | bytes 98312 | tf_op jit(solution)/shard_map/ppermute | solution.py:27
  17.9 1.9 collective-permute-start
  19.8 1.3 collective-permute-start.3
  22.4 6.9 %collective-permute-done.3 = f32[2,8,1,128]{3,1,2,0:T(8,128)S(1)} collective-permute-done((f32[2,8,1,128]{3,1,2,0:T(8,128)S(1)}, f32[2,8,1,128]{3,1,2,0:T(8,128)S(1)}, u32[]{:S(2)}, u32[]{:S(2)}) %collective-permute-start.3) | collective-permute-done | bytes 8224 | tf_op jit(solution)/shard_map/ppermute | solution.py:27
  29.8 3.1 collective-permute-start.5
  33.2 1.9 collective-permute-start.7
  35.1 5.8 %collective-permute-start.2 = (f32[1,1,32,128]{3,2,1,0:T(8,128)S(1)}, f32[1,1,32,128]{3,2,1,0:T(8,128)S(1)}, u32[]{:S(2)}, u32[]{:S(2)}) collective-permute-start(f32[1,1,32,128]{3,2,1,0:T(8,128)S(1)} %slice_bitcast_fusion.30), channel_id=1, source_target_pairs={{8,0},{16,8},{24,16},{32,24},{40,32},{48,40},{56,48},{64,56},{72,6... | collective-permute-start | bytes 49160 | tf_op jit(solution)/shard_map/ppermute | solution.py:27
  40.8 1.3 collective-permute-start.8
  42.5 1.3 collective-permute-start.11
  43.8 6.4 %collective-permute-done.8 = f32[1,8,1,128]{3,1,2,0:T(8,128)S(1)} collective-permute-done((f32[1,8,1,128]{3,1,2,0:T(8,128)S(1)}, f32[1,8,1,128]{3,1,2,0:T(8,128)S(1)}, u32[]{:S(2)}, u32[]{:S(2)}) %collective-permute-start.8) | collective-permute-done | bytes 4128 | tf_op jit(solution)/shard_map/ppermute | solution.py:27
  50.7 1.9 collective-permute-start.12
  52.6 8.5 %collective-permute-start.9 = (f32[1,8,1,128]{3,1,2,0:T(8,128)S(1)}, f32[1,8,1,128]{3,1,2,0:T(8,128)S(1)}, u32[]{:S(2)}, u32[]{:S(2)}) collective-permute-start(f32[1,8,1,128]{3,1,2,0:T(8,128)S(1)} %bitcast.475), channel_id=1, source_target_pairs={{0,1},{1,2},{2,3},{3,4},{4,5},{5,6},{6,7},{8,9},{9,10},{10,11},{11... | collective-permute-start | bytes 12296 | tf_op jit(solution)/shard_map/ppermute | solution.py:27
  61.1 2.1 collective-permute-start.6
  63.3 5.0 %collective-permute-done.6 = f32[1,1,32,128]{3,2,1,0:T(8,128)S(1)} collective-permute-done((f32[1,1,32,128]{3,2,1,0:T(8,128)S(1)}, f32[1,1,32,128]{3,2,1,0:T(8,128)S(1)}, u32[]{:S(2)}, u32[]{:S(2)}) %collective-permute-start.6) | collective-permute-done | bytes 16416 | tf_op jit(solution)/shard_map/ppermute | solution.py:27
  68.7 5.6 %collective-permute-start.13 = (f32[2,8,1,128]{3,1,2,0:T(8,128)S(1)}, f32[2,8,1,128]{3,1,2,0:T(8,128)S(1)}, u32[]{:S(2)}, u32[]{:S(2)}) collective-permute-start(f32[2,8,1,128]{3,1,2,0:T(8,128)S(1)} %pad_maximum_fusion.15), channel_id=1, source_target_pairs={{0,1},{1,2},{2,3},{3,4},{4,5},{5,6},{6,7},{8,9},{9,10},{10,11},{11... | collective-permute-start | bytes 24584 | tf_op jit(solution)/shard_map/ppermute | solution.py:27
  74.4 1.9 collective-permute-start.14
  76.4 1.3 collective-permute-start.15
  77.8 5.8 %collective-permute-start.10 = (f32[1,1,32,128]{3,2,1,0:T(8,128)S(1)}, f32[1,1,32,128]{3,2,1,0:T(8,128)S(1)}, u32[]{:S(2)}, u32[]{:S(2)}) collective-permute-start(f32[1,1,32,128]{3,2,1,0:T(8,128)S(1)} %slice_bitcast_fusion.22), channel_id=1, source_target_pairs={{8,0},{16,8},{24,16},{32,24},{40,32},{48,40},{56,48},{64,56},{72,6... | collective-permute-start | bytes 49160 | tf_op jit(solution)/shard_map/ppermute | solution.py:27
  83.6 2.2 collective-permute-done.15
  87.9 1.2 pad_maximum_fusion.2
  89.0 8.9 %all-to-all-start = ((f32[2,3,1,72,256]{4,0,2,1,3:T(2,128)}), f32[2,3,1,72,256]{4,0,2,1,3:T(2,128)S(1)}, u32[]{:S(2)}, u32[]{:S(2)}) async-start(f32[2,3,1,72,256]{4,0,2,1,3:T(2,128)} %pad_maximum_fusion.2), calls=%async_computation | async-start | bytes 884736 | tf_op jit(solution)/shard_map/all_to_all | solution.py:172
  98.0 14.3 %all-to-all-done = f32[2,3,1,72,256]{4,0,2,1,3:T(2,128)S(1)} async-done(((f32[2,3,1,72,256]{4,0,2,1,3:T(2,128)}), f32[2,3,1,72,256]{4,0,2,1,3:T(2,128)S(1)}, u32[]{:S(2)}, u32[]{:S(2)}) %all-to-all-start) | async-done | bytes 442400 | tf_op jit(solution)/shard_map/all_to_all | solution.py:172
  112.3 1.3 slice_reduce_fusion.5
  113.9 2.9 fusion.36
  116.8 2.9 fusion.39
  120.0 2.9 fusion.24
  122.9 3.1 fusion.33
  126.4 1.8 copy.164
  128.2 8.0 %all-to-all-start.1 = ((f32[2,3,1,256,72]{4,2,1,0,3:T(1,128)}), f32[2,3,1,256,72]{4,2,1,0,3:T(1,128)S(1)}, u32[]{:S(2)}, u32[]{:S(2)}) async-start(f32[2,3,1,256,72]{4,2,1,0,3:T(1,128)} %copy.164), calls=%async_computation.1 | async-start | bytes 1572864 | tf_op jit(solution)/shard_map/all_to_all | solution.py:180
  136.4 21.7 %all-to-all-done.1 = f32[2,3,1,256,72]{4,2,1,0,3:T(1,128)S(1)} async-done(((f32[2,3,1,256,72]{4,2,1,0,3:T(1,128)}), f32[2,3,1,256,72]{4,2,1,0,3:T(1,128)S(1)}, u32[]{:S(2)}, u32[]{:S(2)}) %all-to-all-start.1) | async-done | bytes 442400 | tf_op jit(solution)/shard_map/all_to_all | solution.py:180
  158.1 2.4 slice_reduce_fusion.3
  160.4 3.7 %reshape.519 = f32[3,64,4,9,8]{4,3,0,2,1:T(8,128)} reshape(f32[3,256,72]{2,0,1:T(4,128)S(1)} %get-tuple-element.5) | data formatting | bytes 442368 | tf_op jit(solution)/shard_map/squeeze | solution.py:186
  164.2 5.4 %copy.168 = f32[3,64,4,9,8]{1,3,4,2,0:T(8,128)S(1)} copy(f32[3,64,4,9,8]{4,3,0,2,1:T(8,128)} %reshape.519) | data formatting | bytes 442368 | tf_op jit(solution)/shard_map/squeeze | solution.py:186
  169.6 3.7 %reshape.518 = f32[3,64,4,9,8]{4,3,0,2,1:T(8,128)} reshape(f32[3,256,72]{2,0,1:T(4,128)S(1)} %get-tuple-element.4) | data formatting | bytes 442368 | tf_op jit(solution)/shard_map/squeeze | solution.py:186
  173.3 5.8 %copy.166 = f32[3,64,4,9,8]{1,3,4,2,0:T(8,128)S(1)} copy(f32[3,64,4,9,8]{4,3,0,2,1:T(8,128)} %reshape.518) | data formatting | bytes 442368 | tf_op jit(solution)/shard_map/squeeze | solution.py:186
  179.1 4.9 %convolution_bitcast_fusion.2 = f32[3,4,9,512]{3,2,1,0:T(8,128)S(1)} fusion(f32[3,64,4,9,8]{1,3,4,2,0:T(8,128)S(1)} %copy.168, s32[64,8]{0,1:T(8,128)S(1)} %multiply_add_fusion), kind=kOutput, calls=%fused_computation.20 | convolution fusion | flops 343408640 | bytes 444416 | tf_op jit(solution)/shard_map/cgazl,glk->cazk/dot_general | solution.py:137
  184.0 4.9 %convolution_bitcast_fusion = f32[3,4,9,512]{3,2,1,0:T(8,128)S(1)} fusion(f32[3,64,4,9,8]{1,3,4,2,0:T(8,128)S(1)} %copy.166, s32[64,8]{0,1:T(8,128)S(1)} %multiply_add_fusion), kind=kOutput, calls=%fused_computation.18 | convolution fusion | flops 343408640 | bytes 444416 | tf_op jit(solution)/shard_map/cgazl,glk->cazk/dot_general | solution.py:137
  188.9 5.0 %fusion.49 = f32[1,3,4,9,512]{4,3,2,1,0:T(8,128)S(1)} fusion(f32[3,4,9,512]{3,2,1,0:T(8,128)S(1)} %convolution_bitcast_fusion.2, f32[3,64,4,9,8]{1,3,4,2,0:T(8,128)S(1)} %copy.166, s32[64,8]{0,1:T(8,128)S(1)} %multiply_add_fusion), kind=kOutput, calls=%fused_computation.46 | convolution fusion | flops 343463936 | bytes 665600 | tf_op jit(solution)/shard_map/cgazl,glk->cazk/dot_general | solution.py:137
  194.0 4.9 %fusion.51 = f32[1,3,4,9,512]{4,3,2,1,0:T(8,128)S(1)} fusion(f32[3,4,9,512]{3,2,1,0:T(8,128)S(1)} %convolution_bitcast_fusion, f32[3,64,4,9,8]{1,3,4,2,0:T(8,128)S(1)} %copy.168, s32[64,8]{0,1:T(8,128)S(1)} %multiply_add_fusion), kind=kOutput, calls=%fused_computation.48 | convolution fusion | flops 343463936 | bytes 665600 | tf_op jit(solution)/shard_map/cgazl,glk->cazk/dot_general | solution.py:137
  199.2 5.1 %fusion.71 = f32[512,3,4,9]{0,3,2,1:T(8,128)S(1)} fusion(f32[2,3,4,9,512]{4,3,2,1,0:T(8,128)S(1)} %pad_maximum_fusion), kind=kOutput, calls=%fused_computation.62 | convolution fusion | flops 343408640 | bytes 614400 | tf_op jit(solution)/shard_map/cazk,kx->cxaz/dot_general | solution.py:137
  204.3 5.3 %fusion.69 = f32[512,3,4,9]{0,3,2,1:T(8,128)S(1)} fusion(f32[2,3,4,9,512]{4,3,2,1,0:T(8,128)S(1)} %pad_maximum_fusion), kind=kOutput, calls=%fused_computation.60 | convolution fusion | flops 343408640 | bytes 614400 | tf_op jit(solution)/shard_map/cazk,kx->cxaz/dot_general | solution.py:137
  209.7 5.2 %fusion.43 = f32[3,512,4,9]{1,3,2,0:T(8,128)S(1)} fusion(f32[512,3,4,9]{0,3,2,1:T(8,128)S(1)} %fusion.71, f32[2,3,4,9,512]{4,3,2,1,0:T(8,128)S(1)} %pad_maximum_fusion), kind=kOutput, calls=%fused_computation.35 | convolution fusion | flops 343463936 | bytes 1007616 | tf_op jit(solution)/shard_map/cazk,kx->cxaz/dot_general | solution.py:137
  215.0 5.2 %fusion.42 = f32[3,512,4,9]{1,3,2,0:T(8,128)S(1)} fusion(f32[512,3,4,9]{0,3,2,1:T(8,128)S(1)} %fusion.69, f32[2,3,4,9,512]{4,3,2,1,0:T(8,128)S(1)} %pad_maximum_fusion), kind=kOutput, calls=%fused_computation.33 | convolution fusion | flops 343463936 | bytes 1007616 | tf_op jit(solution)/shard_map/cazk,kx->cxaz/dot_general | solution.py:137
  220.5 1.2 copy.173
  221.7 3.9 %reshape.528 = f32[64,1,1728]{2,1,0:T(1,128)} reshape(f32[512,3,1,2,36]{4,3,2,1,0:T(2,128)S(1)} %bitcast.428) | data formatting | bytes 884736
  225.6 7.6 %all-to-all-start.2 = ((f32[64,1,1728]{2,1,0:T(1,128)}), f32[64,1,1728]{2,1,0:T(1,128)S(1)}, u32[]{:S(2)}, u32[]{:S(2)}) async-start(f32[64,1,1728]{2,1,0:T(1,128)} %reshape.528), calls=%async_computation.2 | async-start | bytes 917504 | tf_op jit(solution)/shard_map/all_to_all | solution.py:224
  233.2 15.2 %all-to-all-done.2 = f32[64,1,1728]{2,1,0:T(1,128)S(1)} async-done(((f32[64,1,1728]{2,1,0:T(1,128)}), f32[64,1,1728]{2,1,0:T(1,128)S(1)}, u32[]{:S(2)}, u32[]{:S(2)}) %all-to-all-start.2) | async-done | bytes 442400 | tf_op jit(solution)/shard_map/all_to_all | solution.py:224
  249.0 1.7 reduce.12
  250.7 2.8 reshape.529
  253.5 6.2 %slice_reduce_fusion = (f32[3,512,36]{2,0,1:T(4,128)}, f32[3,512,36]{2,0,1:T(4,128)}) fusion(f32[2,3,1,512,36]{4,0,2,1,3:T(2,128)S(1)} %bitcast.427), kind=kLoop, calls=%fused_computation.94 | loop fusion | bytes 884736 | tf_op jit(solution)/shard_map/slice | solution.py:230
  259.7 3.0 reshape.520
  262.7 3.0 copy.175
  265.7 3.0 reshape.521
  268.7 3.1 copy.177
  271.8 2.9 convolution_bitcast_fusion.7
  274.7 2.9 convolution_bitcast_fusion.5
  277.7 1.7 fusion.47
  279.6 1.7 fusion.45
  288.0 3.8 %all-to-all-start.3 = ((f32[8,2,3,1,32,72]{5,4,3,2,1,0:T(8,128)}), f32[8,2,3,1,32,72]{5,4,3,2,1,0:T(8,128)S(1)}, u32[]{:S(2)}, u32[]{:S(2)}) async-start(f32[8,2,3,1,32,72]{5,4,3,2,1,0:T(8,128)} %constant_dynamic-update-slice_fusion), calls=%async_computation.3 | async-start | bytes 1572864 | tf_op jit(solution)/shard_map/all_to_all | solution.py:14
  291.8 26.1 %all-to-all-done.3 = f32[8,2,3,1,32,72]{5,4,3,2,1,0:T(8,128)S(1)} async-done(((f32[8,2,3,1,32,72]{5,4,3,2,1,0:T(8,128)}), f32[8,2,3,1,32,72]{5,4,3,2,1,0:T(8,128)S(1)}, u32[]{:S(2)}, u32[]{:S(2)}) %all-to-all-start.3) | async-done | bytes 442400 | tf_op jit(solution)/shard_map/all_to_all | solution.py:14
  318.5 2.8 fusion.12
  321.4 3.5 %multiply_reduce_fusion = (f32[8,32,128]{2,1,0:T(8,128)}, f32[8,32,128]{2,1,0:T(8,128)}) fusion(bf16[3,8,32,128]{3,2,1,0:T(8,128)(2,1)S(1)} %copy-done.7, f32[1,8,32,128]{3,2,1,0:T(8,128)S(1)} %get-tuple-element.44, f32[1,8,32,128]{3,2,1,0:T(8,128)S(1)} %fusion.202, f32[1,8,32,128]{3,2,1,0:T(8,128)S(1)} %get-tuple-element.43, ...), kind=kOutput, calls=%fused_computation.109 | convolution fusion | flops 86088704 | bytes 1663552 | tf_op jit(solution)/shard_map/cgybx,gbn->cxyn/dot_general | solution.py:137
  (148 shorter events, 16.5 us)
Async XLA Ops:
  0.6 28.7 %copy-start = (f32[3,8,32,128]{3,2,1,0:T(8,128)S(1)}, f32[3,8,32,128]{3,2,1,0:T(8,128)}, u32[]{:S(2)}) copy-start(f32[3,8,32,128]{3,2,1,0:T(8,128)} %param.7) | copy-start | bytes 1179652
  0.6 28.7 %copy-start.3 = (bf16[8,32,128]{2,1,0:T(8,128)(2,1)S(1)}, bf16[8,32,128]{2,1,0:T(8,128)(2,1)}, u32[]{:S(2)}) copy-start(bf16[8,32,128]{2,1,0:T(8,128)(2,1)} %param.10) | copy-start | bytes 196612
  0.7 28.7 %copy-start.5 = (f32[6,8,32,128]{3,2,1,0:T(8,128)S(1)}, f32[6,8,32,128]{3,2,1,0:T(8,128)}, u32[]{:S(2)}) copy-start(f32[6,8,32,128]{3,2,1,0:T(8,128)} %param.8) | copy-start | bytes 2359300
  1.8 27.6 %copy-start.6 = (bf16[8,32,128]{2,1,0:T(8,128)(2,1)S(1)}, bf16[8,32,128]{2,1,0:T(8,128)(2,1)}, u32[]{:S(2)}) copy-start(bf16[8,32,128]{2,1,0:T(8,128)(2,1)} %param.9) | copy-start | bytes 196612
  1.8 27.6 %collective-permute-start.1 = (f32[1,8,1,128]{3,1,2,0:T(8,128)S(1)}, f32[1,8,1,128]{3,1,2,0:T(8,128)S(1)}, u32[]{:S(2)}, u32[]{:S(2)}) collective-permute-start(f32[1,8,1,128]{3,1,2,0:T(8,128)S(1)} %bitcast.474), channel_id=1, source_target_pairs={{0,1},{1,2},{2,3},{3,4},{4,5},{5,6},{6,7},{8,9},{9,10},{10,11},{11... | collective-permute-start | bytes 12296 | tf_op jit(solution)/shard_map/ppermute | solution.py:27
  12.6 16.7 %collective-permute-start.4 = (f32[2,1,32,128]{3,2,1,0:T(8,128)S(1)}, f32[2,1,32,128]{3,2,1,0:T(8,128)S(1)}, u32[]{:S(2)}, u32[]{:S(2)}) collective-permute-start(f32[2,1,32,128]{3,2,1,0:T(8,128)S(1)} %stack.161), channel_id=1, source_target_pairs={{8,0},{16,8},{24,16},{32,24},{40,32},{48,40},{56,48},{64,56},{72,6... | collective-permute-start | bytes 98312 | tf_op jit(solution)/shard_map/ppermute | solution.py:27
  17.9 11.6 %collective-permute-start = (f32[1,1,32,128]{3,2,1,0:T(8,128)S(1)}, f32[1,1,32,128]{3,2,1,0:T(8,128)S(1)}, u32[]{:S(2)}, u32[]{:S(2)}) collective-permute-start(f32[1,1,32,128]{3,2,1,0:T(8,128)S(1)} %slice.325), channel_id=1, source_target_pairs={{0,8},{8,16},{16,24},{24,32},{32,40},{40,48},{48,56},{56,64},{64,7... | collective-permute-start | bytes 49160 | tf_op jit(solution)/shard_map/ppermute | solution.py:27
  19.8 9.5 %collective-permute-start.3 = (f32[2,8,1,128]{3,1,2,0:T(8,128)S(1)}, f32[2,8,1,128]{3,1,2,0:T(8,128)S(1)}, u32[]{:S(2)}, u32[]{:S(2)}) collective-permute-start(f32[2,8,1,128]{3,1,2,0:T(8,128)S(1)} %pad_maximum_fusion.12), channel_id=1, source_target_pairs={{1,0},{2,1},{3,2},{4,3},{5,4},{6,5},{7,6},{9,8},{10,9},{11,10},{12... | collective-permute-start | bytes 24584 | tf_op jit(solution)/shard_map/ppermute | solution.py:27
  29.6 12.6 %copy-start.4 = (bf16[8,32,128]{2,1,0:T(8,128)(2,1)S(1)}, bf16[8,32,128]{2,1,0:T(8,128)(2,1)}, u32[]{:S(2)}) copy-start(bf16[8,32,128]{2,1,0:T(8,128)(2,1)} %param.11) | copy-start | bytes 196612
  29.8 12.3 %collective-permute-start.5 = (f32[2,8,1,128]{3,1,2,0:T(8,128)S(1)}, f32[2,8,1,128]{3,1,2,0:T(8,128)S(1)}, u32[]{:S(2)}, u32[]{:S(2)}) collective-permute-start(f32[2,8,1,128]{3,1,2,0:T(8,128)S(1)} %pad_maximum_fusion.13), channel_id=1, source_target_pairs={{0,1},{1,2},{2,3},{3,4},{4,5},{5,6},{6,7},{8,9},{9,10},{10,11},{11... | collective-permute-start | bytes 24584 | tf_op jit(solution)/shard_map/ppermute | solution.py:27
  33.2 9.0 %collective-permute-start.7 = (f32[2,1,32,128]{3,2,1,0:T(8,128)S(1)}, f32[2,1,32,128]{3,2,1,0:T(8,128)S(1)}, u32[]{:S(2)}, u32[]{:S(2)}) collective-permute-start(f32[2,1,32,128]{3,2,1,0:T(8,128)S(1)} %pad_maximum_fusion.9), channel_id=1, source_target_pairs={{0,8},{8,16},{16,24},{24,32},{32,40},{40,48},{48,56},{56,64},{64,7... | collective-permute-start | bytes 98312 | tf_op jit(solution)/shard_map/ppermute | solution.py:27
  35.1 7.2 %collective-permute-start.2 = (f32[1,1,32,128]{3,2,1,0:T(8,128)S(1)}, f32[1,1,32,128]{3,2,1,0:T(8,128)S(1)}, u32[]{:S(2)}, u32[]{:S(2)}) collective-permute-start(f32[1,1,32,128]{3,2,1,0:T(8,128)S(1)} %slice_bitcast_fusion.30), channel_id=1, source_target_pairs={{8,0},{16,8},{24,16},{32,24},{40,32},{48,40},{56,48},{64,56},{72,6... | collective-permute-start | bytes 49160 | tf_op jit(solution)/shard_map/ppermute | solution.py:27
  40.8 9.4 %collective-permute-start.8 = (f32[1,8,1,128]{3,1,2,0:T(8,128)S(1)}, f32[1,8,1,128]{3,1,2,0:T(8,128)S(1)}, u32[]{:S(2)}, u32[]{:S(2)}) collective-permute-start(f32[1,8,1,128]{3,1,2,0:T(8,128)S(1)} %bitcast.473), channel_id=1, source_target_pairs={{1,0},{2,1},{3,2},{4,3},{5,4},{6,5},{7,6},{9,8},{10,9},{11,10},{12... | collective-permute-start | bytes 12296 | tf_op jit(solution)/shard_map/ppermute | solution.py:27
  42.5 20.7 %collective-permute-start.11 = (f32[2,8,1,128]{3,1,2,0:T(8,128)S(1)}, f32[2,8,1,128]{3,1,2,0:T(8,128)S(1)}, u32[]{:S(2)}, u32[]{:S(2)}) collective-permute-start(f32[2,8,1,128]{3,1,2,0:T(8,128)S(1)} %pad_maximum_fusion.14), channel_id=1, source_target_pairs={{1,0},{2,1},{3,2},{4,3},{5,4},{6,5},{7,6},{9,8},{10,9},{11,10},{12... | collective-permute-start | bytes 24584 | tf_op jit(solution)/shard_map/ppermute | solution.py:27
  50.7 12.6 %collective-permute-start.12 = (f32[2,1,32,128]{3,2,1,0:T(8,128)S(1)}, f32[2,1,32,128]{3,2,1,0:T(8,128)S(1)}, u32[]{:S(2)}, u32[]{:S(2)}) collective-permute-start(f32[2,1,32,128]{3,2,1,0:T(8,128)S(1)} %pad_maximum_fusion.10), channel_id=1, source_target_pairs={{8,0},{16,8},{24,16},{32,24},{40,32},{48,40},{56,48},{64,56},{72,6... | collective-permute-start | bytes 98312 | tf_op jit(solution)/shard_map/ppermute | solution.py:27
  52.6 10.7 %collective-permute-start.9 = (f32[1,8,1,128]{3,1,2,0:T(8,128)S(1)}, f32[1,8,1,128]{3,1,2,0:T(8,128)S(1)}, u32[]{:S(2)}, u32[]{:S(2)}) collective-permute-start(f32[1,8,1,128]{3,1,2,0:T(8,128)S(1)} %bitcast.475), channel_id=1, source_target_pairs={{0,1},{1,2},{2,3},{3,4},{4,5},{5,6},{6,7},{8,9},{9,10},{10,11},{11... | collective-permute-start | bytes 12296 | tf_op jit(solution)/shard_map/ppermute | solution.py:27
  61.1 7.2 %collective-permute-start.6 = (f32[1,1,32,128]{3,2,1,0:T(8,128)S(1)}, f32[1,1,32,128]{3,2,1,0:T(8,128)S(1)}, u32[]{:S(2)}, u32[]{:S(2)}) collective-permute-start(f32[1,1,32,128]{3,2,1,0:T(8,128)S(1)} %slice_bitcast_fusion.27), channel_id=1, source_target_pairs={{0,8},{8,16},{16,24},{24,32},{32,40},{40,48},{48,56},{56,64},{64,7... | collective-permute-start | bytes 49160 | tf_op jit(solution)/shard_map/ppermute | solution.py:27
  68.7 14.8 %collective-permute-start.13 = (f32[2,8,1,128]{3,1,2,0:T(8,128)S(1)}, f32[2,8,1,128]{3,1,2,0:T(8,128)S(1)}, u32[]{:S(2)}, u32[]{:S(2)}) collective-permute-start(f32[2,8,1,128]{3,1,2,0:T(8,128)S(1)} %pad_maximum_fusion.15), channel_id=1, source_target_pairs={{0,1},{1,2},{2,3},{3,4},{4,5},{5,6},{6,7},{8,9},{9,10},{10,11},{11... | collective-permute-start | bytes 24584 | tf_op jit(solution)/shard_map/ppermute | solution.py:27
  74.4 9.1 %collective-permute-start.14 = (f32[2,1,32,128]{3,2,1,0:T(8,128)S(1)}, f32[2,1,32,128]{3,2,1,0:T(8,128)S(1)}, u32[]{:S(2)}, u32[]{:S(2)}) collective-permute-start(f32[2,1,32,128]{3,2,1,0:T(8,128)S(1)} %pad_maximum_fusion.11), channel_id=1, source_target_pairs={{0,8},{8,16},{16,24},{24,32},{32,40},{40,48},{48,56},{56,64},{64,7... | collective-permute-start | bytes 98312 | tf_op jit(solution)/shard_map/ppermute | solution.py:27
  76.4 9.4 %collective-permute-start.15 = (f32[1,8,1,128]{3,1,2,0:T(8,128)S(1)}, f32[1,8,1,128]{3,1,2,0:T(8,128)S(1)}, u32[]{:S(2)}, u32[]{:S(2)}) collective-permute-start(f32[1,8,1,128]{3,1,2,0:T(8,128)S(1)} %bitcast.476), channel_id=1, source_target_pairs={{1,0},{2,1},{3,2},{4,3},{5,4},{6,5},{7,6},{9,8},{10,9},{11,10},{12... | collective-permute-start | bytes 12296 | tf_op jit(solution)/shard_map/ppermute | solution.py:27
  77.8 8.1 %collective-permute-start.10 = (f32[1,1,32,128]{3,2,1,0:T(8,128)S(1)}, f32[1,1,32,128]{3,2,1,0:T(8,128)S(1)}, u32[]{:S(2)}, u32[]{:S(2)}) collective-permute-start(f32[1,1,32,128]{3,2,1,0:T(8,128)S(1)} %slice_bitcast_fusion.22), channel_id=1, source_target_pairs={{8,0},{16,8},{24,16},{32,24},{40,32},{48,40},{56,48},{64,56},{72,6... | collective-permute-start | bytes 49160 | tf_op jit(solution)/shard_map/ppermute | solution.py:27
  89.0 23.3 %all-to-all-start = ((f32[2,3,1,72,256]{4,0,2,1,3:T(2,128)}), f32[2,3,1,72,256]{4,0,2,1,3:T(2,128)S(1)}, u32[]{:S(2)}, u32[]{:S(2)}) async-start(f32[2,3,1,72,256]{4,0,2,1,3:T(2,128)} %pad_maximum_fusion.2), calls=%async_computation | async-start | bytes 884736 | tf_op jit(solution)/shard_map/all_to_all | solution.py:172
  128.2 29.9 %all-to-all-start.1 = ((f32[2,3,1,256,72]{4,2,1,0,3:T(1,128)}), f32[2,3,1,256,72]{4,2,1,0,3:T(1,128)S(1)}, u32[]{:S(2)}, u32[]{:S(2)}) async-start(f32[2,3,1,256,72]{4,2,1,0,3:T(1,128)} %copy.164), calls=%async_computation.1 | async-start | bytes 1572864 | tf_op jit(solution)/shard_map/all_to_all | solution.py:180
  225.6 22.8 %all-to-all-start.2 = ((f32[64,1,1728]{2,1,0:T(1,128)}), f32[64,1,1728]{2,1,0:T(1,128)S(1)}, u32[]{:S(2)}, u32[]{:S(2)}) async-start(f32[64,1,1728]{2,1,0:T(1,128)} %reshape.528), calls=%async_computation.2 | async-start | bytes 917504 | tf_op jit(solution)/shard_map/all_to_all | solution.py:224
  271.8 5.9 %copy-start.2 = (f32[3,64,8,4,9]{1,4,3,2,0:T(8,128)S(1)}, f32[3,64,8,4,9]{1,4,3,2,0:T(8,128)}, u32[]{:S(2)}) copy-start(f32[3,64,8,4,9]{1,4,3,2,0:T(8,128)} %copy.177) | copy-start | bytes 663556
  274.7 4.9 %copy-start.1 = (f32[3,64,8,4,9]{1,4,3,2,0:T(8,128)S(1)}, f32[3,64,8,4,9]{1,4,3,2,0:T(8,128)}, u32[]{:S(2)}) copy-start(f32[3,64,8,4,9]{1,4,3,2,0:T(8,128)} %copy.175) | copy-start | bytes 663556
  288.0 29.9 %all-to-all-start.3 = ((f32[8,2,3,1,32,72]{5,4,3,2,1,0:T(8,128)}), f32[8,2,3,1,32,72]{5,4,3,2,1,0:T(8,128)S(1)}, u32[]{:S(2)}, u32[]{:S(2)}) async-start(f32[8,2,3,1,32,72]{5,4,3,2,1,0:T(8,128)} %constant_dynamic-update-slice_fusion), calls=%async_computation.3 | async-start | bytes 1572864 | tf_op jit(solution)/shard_map/all_to_all | solution.py:14
  318.5 2.9 copy-start.7
  318.5 2.8 copy-start.8
